TPU v7x, 256 devices: a whole 4x4x8 slice. The times are simulated.
256 devices in a mesh: dom: 128 (over z, y, x), ord: 2 (over core).
Axes of the slice: x: 4, y: 4, z: 8, core: 2. Of those that a mesh axis runs over, the one named last changes fastest.
Arguments:
- polar_images: bfloat16 [1024, 128, 512], P(('dom', 'ord')), may hold values from -6 to 6
- radial_basis: bfloat16 [256, 128, 128], P('ord'), may hold values from -0.5 to 0.5
- radial_start: int32 [256], P('ord'), may hold values from 0 to 4, as said below
- radial_count: int32 [256], P('ord'), may hold values from 32 to 128
- order_of_slot: int32 [256], replicated, may hold values from 0 to 255, each once
- start_block: float32 [256, 16, 128], P('ord'), may hold values from -6 to 6
Outputs:
- denoised: bfloat16 [1024, 128, 512], P(('dom', 'ord'))
Inputs may be any that keep to these rules, and one draw needn't show every extreme that they name: `radial_start`: every slot keeps at least 64 radial samples.
All inputs are finite; a program needn't handle non-finite values.
Results may differ from a plain program's by a relative error of at most 0.01.
Values may be sent and summed in bfloat16 or wider, within the bound.
A program may use at most 64 MiB of HBM per device.

v0:
```python
import math
import jax
import jax.numpy as jnp
from jax import lax
from jax.sharding import PartitionSpec as P

NRB = 8
ITERS = 4


def make_table(order_of_slot, angles):
    steps_t = jnp.arange(angles, dtype=jnp.int32)
    phase_int = steps_t[:, None] * order_of_slot[None, :] % angles
    radians = phase_int.astype(jnp.float32) * (2.0 * math.pi / angles)
    weight = math.sqrt(2.0 / angles)
    paired = jnp.stack([jnp.cos(radians) * weight, -jnp.sin(radians) * weight], axis=2)
    return paired.reshape(angles, -1).astype(jnp.bfloat16)


def masked_basis(radial_basis, radial_start, radial_count, blocks):
    radial_rows = radial_basis.shape[1]
    slot_cols = radial_basis.shape[2]
    row_ids = jnp.arange(radial_rows, dtype=jnp.int32)
    col_ids = jnp.arange(slot_cols, dtype=jnp.int32)
    keep_rows = row_ids[None, :, None] >= radial_start[:, None, None] * (radial_rows // blocks)
    keep_cols = col_ids[None, None, :] < radial_count[:, None, None]
    return jnp.where(keep_rows & keep_cols, radial_basis, jnp.zeros_like(radial_basis))


def orthonormal(image_t):
    gram_matrix = jnp.einsum("srq,stq->srt", image_t, image_t, precision=lax.Precision.HIGHEST)
    factor = jnp.linalg.cholesky(gram_matrix)
    return jax.scipy.linalg.solve_triangular(factor, image_t, lower=True)


def subspace(cov_mat, start_t):
    basis_t = start_t
    for step in range(ITERS):
        image_t = jnp.einsum("srm,smq->srq", basis_t, cov_mat, precision=lax.Precision.HIGHEST)
        basis_t = orthonormal(image_t)
    return basis_t


def radial_images(eig_t, masked):
    return jnp.einsum("stq,srq->str", eig_t, masked, preferred_element_type=jnp.float32).astype(
        jnp.bfloat16
    )


def on_device(polar_images, radial_basis, radial_start, radial_count, order_of_slot, start_block):
    particles, radial_rows, angles = polar_images.shape
    dft_table = make_table(order_of_slot, angles)
    spectrum = jnp.dot(
        polar_images.reshape(particles * radial_rows, angles),
        dft_table,
        preferred_element_type=jnp.float32,
    )
    spectrum = spectrum.astype(jnp.bfloat16).reshape(particles, radial_rows, -1)
    regrouped = lax.all_to_all(spectrum, "ord", split_axis=2, concat_axis=0, tiled=True)
    owned_slots = radial_basis.shape[0]
    group_rows = regrouped.shape[0]
    local_spec = regrouped.reshape(group_rows, radial_rows, owned_slots, 2)
    masked = masked_basis(radial_basis, radial_start, radial_count, NRB)
    coef_four = jnp.einsum(
        "prsc,srq->scpq", local_spec, masked, preferred_element_type=jnp.float32
    ).astype(jnp.bfloat16)
    coef_rows = coef_four.reshape(owned_slots, 2 * group_rows, -1)
    partial_value = jnp.einsum(
        "snq,snm->sqm", coef_rows, coef_rows, preferred_element_type=jnp.float32
    )
    cov_mine = lax.psum_scatter(partial_value, "dom", scatter_dimension=0, tiled=True)
    share_count = cov_mine.shape[0]
    first_slot = lax.axis_index("dom") * share_count
    mine_start = lax.dynamic_slice_in_dim(start_block, first_slot, share_count, 0)
    mine_basis = lax.dynamic_slice_in_dim(masked, first_slot, share_count, 0)
    eig_mine = subspace(cov_mine, mine_start).astype(jnp.bfloat16)
    u_mine = radial_images(eig_mine, mine_basis)
    eig_t, u_t = (
        lax.all_gather(eig_mine, "dom", axis=0, tiled=True),
        lax.all_gather(u_mine, "dom", axis=0, tiled=True),
    )
    scores = jnp.einsum(
        "scpq,stq->psct", coef_four, eig_t, preferred_element_type=jnp.float32
    ).astype(jnp.bfloat16)
    local_profile = jnp.einsum(
        "psct,str->prsc", scores, u_t, preferred_element_type=jnp.float32
    ).astype(jnp.bfloat16)
    local_profile = local_profile.reshape(group_rows, radial_rows, -1)
    profile = lax.all_to_all(local_profile, "ord", split_axis=0, concat_axis=2, tiled=True).reshape(
        particles * radial_rows, -1
    )
    denoised = lax.dot_general(
        profile, dft_table, (((1,), (1,)), ((), ())), preferred_element_type=jnp.float32
    )
    return denoised.astype(jnp.bfloat16).reshape(particles, radial_rows, angles)


def solution(mesh):
    placed = (
        P(("dom", "ord"), None, None),
        P("ord", None, None),
        P("ord"),
        P("ord"),
        P(),
        P("ord", None, None),
    )
    return jax.shard_map(
        on_device,
        mesh=mesh,
        in_specs=placed,
        out_specs=P(("dom", "ord"), None, None),
        check_vma=False,
    )
```

profile of v0, /device:TPU:1, one launch (start us, length us, event | category | flops | bytes accessed | tf_op | source)
XLA Modules:
  0.0 1476.3 jit_solution(6241815372960781831)
XLA Ops:
  6.5 0.0 copy-start
  6.5 0.0 copy-start.3
  6.5 3.0 multiply_convert_fusion.1
  9.6 0.1 pad_maximum_fusion
  9.7 0.5 copy.48
  10.2 0.2 convert_element_type.65
  10.4 1.5 convolution_convert_fusion.3
  11.9 1.1 copy.49
  13.0 6.7 all-to-all-start
  19.6 0.0 reduce-scatter.2.cloned.1.call-start
  19.6 0.0 copy-done.3
  19.6 1.4 all-to-all-done
  21.0 0.2 copy.50
  21.2 0.0 copy-done.2
  21.2 0.1 iota_compare_fusion
  21.3 6.0 and_select_fusion
  27.4 0.0 copy-start.1
  27.4 2.0 copy-done.1
  29.3 1.2 fusion.2
  30.5 4.5 fusion.12
  35.1 0.0 reduce-scatter.2.cloned.1.call-update
  35.1 620.3 %reduce-scatter.2.cloned.1.call-done = f32[1,128,128]{2,1,0:T(8,128)} async-done(((f32[128,128,128]{2,1,0:T(8,128)}), f32[1,128,128]{2,1,0:T(8,128)}) %reduce-scatter.2.cloned.1.call-update) | async-done | bytes 65552 | tf_op jit(solution)/shard_map/reduce_scatter | solution.py:71
  655.4 0.0 copy-done
  655.4 1.0 fusion.25
  656.4 0.1 fusion.51
  656.5 0.1 copy.52
  656.6 1.5 custom-call.12
  658.1 0.6 compare_reduce_fusion.3
  658.8 0.6 select_select_fusion.3
  659.4 1.2 custom-call.13
  660.6 0.2 fusion.38
  660.8 1.0 fusion.23
  661.8 0.1 fusion.52
  662.0 0.1 copy.54
  662.1 1.5 custom-call.14
  663.6 0.6 compare_reduce_fusion.2
  664.2 0.6 select_select_fusion.2
  664.9 1.2 custom-call.15
  666.1 0.2 fusion.36
  666.3 1.0 fusion.21
  667.3 0.1 fusion.53
  667.5 0.1 copy.56
  667.5 1.5 custom-call.16
  669.0 0.6 compare_reduce_fusion.1
  669.7 0.6 select_select_fusion.1
  670.3 1.2 custom-call.17
  671.6 0.2 fusion.34
  671.8 1.0 fusion.19
  672.8 0.1 fusion.54
  672.9 0.1 copy.58
  673.0 1.5 custom-call.18
  674.5 0.6 compare_reduce_fusion
  675.2 0.6 select_select_fusion
  675.8 1.2 custom-call.19
  677.0 0.2 fusion.6
  677.2 0.9 convolution_convert_fusion.4
  678.1 287.7 %all_gather.7 = bf16[128,16,128]{2,1,0:T(8,128)(2,1)S(1)} all-gather(bf16[1,16,128]{2,1,0:T(8,128)(2,1)S(1)} %fusion.6), channel_id=1, replica_groups=mesh['dom'=128,'ord'=2] {'dom'}, dimensions={0}, use_global_device_ids=true | all-gather | bytes 528384 | tf_op jit(solution)/shard_map/all_gather | solution.py:79
  965.9 285.6 %all-gather = bf16[2048,128]{1,0:T(8,128)(2,1)S(1)} all-gather(bf16[16,128]{1,0:T(8,128)(2,1)S(1)} %convolution_convert_fusion.4), channel_id=2, replica_groups=mesh['dom'=128,'ord'=2] {'dom'}, dimensions={0}, use_global_device_ids=true | all-gather | bytes 528384 | tf_op jit(solution)/shard_map/all_gather | solution.py:80
  1251.4 1.3 convolution_convert_fusion.1
  1252.7 1.3 copy.59
  1254.1 213.6 %all_to_all.30 = bf16[8,128,256]{2,1,0:T(8,128)(2,1)S(1)} all-to-all(bf16[8,128,256]{2,1,0:T(8,128)(2,1)S(1)} %copy.59), channel_id=1, replica_groups=mesh['dom'=128,'ord'=2] {'ord'}, dimensions={0} | all-to-all | bytes 1048576 | tf_op jit(solution)/shard_map/all_to_all | solution.py:89
  1467.6 0.5 copy.60
  1468.2 0.1 copy.68
  1468.3 1.2 convolution_convert_fusion
  (10 shorter events, 0.2 us)
Async XLA Ops:
  6.5 648.9 %copy-start = (f32[128,16,128]{2,1,0:T(8,128)S(1)}, f32[128,16,128]{2,1,0:T(8,128)}, u32[]{:S(2)}) copy-start(f32[128,16,128]{2,1,0:T(8,128)} %param.14) | copy-start | bytes 3145732
  6.5 13.1 copy-start.3
  6.5 14.7 copy-start.2
  13.0 8.1 all-to-all-start
  19.6 635.7 %reduce-scatter.2.cloned.1.call-start = ((), (), s32[]{:S(2)}) async-start(), calls=%async_computation.3 | async-start | bytes 8454144 | tf_op jit(solution)/shard_map/reduce_scatter | solution.py:71
  27.4 2.0 copy-start.1
Sparse Core Ops, SparseCore 0:
  35.2 620.1 reduce-scatter.1
where the time goes:
time: 1480 us
  blocking collectives  787 us (53%)
  waiting for transfers between devices  622 us (42%)
  other arithmetic  25.4 us (2%)
  matrix products  16.1 us (1%)
    reduce_scatter x1, waiting for transfers between devices, on_device(): lax.psum_scatter(partial_value, 'dom', scatter_dimension=0, tiled=True)  620 us
    all_gather x1, blocking collectives, on_device(): lax.all_gather(eig_mine, 'dom', axis=0, tiled=True)  288 us
    all_gather x1, blocking collectives, on_device(): lax.all_gather(u_mine, 'dom', axis=0, tiled=True)  286 us
    all_to_all x1, blocking collectives, on_device(): lax.all_to_all(local_profile, 'ord', split_axis=0, concat_axis=2, tiled=T...  214 us
  transfers between devices with their start and end apart: 2, of which 2 were waited for; matrix products, arithmetic and copies ran while one was open for 0% of the time, Pallas kernels for 0%

commit v1 on v0

--- a/solution.py
+++ b/solution.py
@@ -76,7 +76,9 @@
     eig_mine = subspace(cov_mine, mine_start).astype(jnp.bfloat16)
     u_mine = radial_images(eig_mine, mine_basis)
     eig_t, u_t = (
-        lax.all_gather(eig_mine, "dom", axis=0, tiled=True),
+        jnp.concatenate(
+            lax.all_to_all(jnp.stack([eig_mine] * lax.axis_size("dom")), "dom", 0, 0), axis=0
+        ),
         lax.all_gather(u_mine, "dom", axis=0, tiled=True),
     )
     scores = jnp.einsum(

time: 1480 us -> 1150 us (0.78)
  blocking collectives: 787 us -> 453 us
    all_gather x1 -> x0, blocking collectives: 288 us -> none  [on_device(): lax.all_gather(eig_mine, 'dom', axis=0, tiled=True)]
    all_to_all x1, blocking collectives: 214 us -> 159 us  [on_device(): lax.all_to_all(local_profile, 'ord', split_axis=0, concat_axis=2, tiled=T...]
  transfers between devices with their start and end apart: 2 -> 3, of which waited for: 2 -> 2; matrix products, arithmetic and copies ran while one was open for 0% -> 0% of each run, Pallas kernels for 0% -> 0%
where the time goes in v1:
time: 1150 us
  waiting for transfers between devices  622 us (54%)
  blocking collectives  453 us (39%)
  other arithmetic  25.4 us (2%)
  matrix products  16.1 us (1%)
  between operations  13.6 us (1%)
  starting transfers between devices  12.9 us (1%)
    reduce_scatter x1, waiting for transfers between devices, on_device(): lax.psum_scatter(partial_value, 'dom', scatter_dimension=0, tiled=True)  620 us
    all_gather x1, blocking collectives, on_device(): lax.all_gather(u_mine, 'dom', axis=0, tiled=True)  294 us
    all_to_all x1, blocking collectives, on_device(): lax.all_to_all(local_profile, 'ord', split_axis=0, concat_axis=2, tiled=T...  159 us
  transfers between devices with their start and end apart: 3, of which 2 were waited for; matrix products, arithmetic and copies ran while one was open for 0% of the time, Pallas kernels for 0%

profile of v1, /device:TPU:1, one launch (start us, length us, event | category | flops | bytes accessed | tf_op | source)
XLA Modules:
  0.0 1149.2 jit_solution(14089253161966752242)
XLA Ops:
  6.5 0.0 copy-start
  6.5 3.0 multiply_convert_fusion.1
  9.6 0.1 pad_maximum_fusion
  9.7 0.5 copy.48
  10.2 0.2 convert_element_type.65
  10.4 1.5 convolution_convert_fusion.3
  11.9 1.1 copy.49
  13.0 6.7 all-to-all-start
  19.6 0.0 reduce-scatter.2.cloned.1.call-start
  19.6 0.0 copy-done.3
  19.6 1.4 all-to-all-done
  21.0 0.2 copy.50
  21.2 0.0 copy-done.2
  21.2 0.1 iota_compare_fusion
  21.3 6.0 and_select_fusion
  27.4 2.0 copy-done.1
  29.3 1.2 fusion.2
  30.5 4.5 fusion.13
  35.1 0.0 reduce-scatter.2.cloned.1.call-update
  35.1 620.3 %reduce-scatter.2.cloned.1.call-done = f32[1,128,128]{2,1,0:T(8,128)} async-done(((f32[128,128,128]{2,1,0:T(8,128)}), f32[1,128,128]{2,1,0:T(8,128)}) %reduce-scatter.2.cloned.1.call-update) | async-done | bytes 65552 | tf_op jit(solution)/shard_map/reduce_scatter | solution.py:71
  655.4 0.0 copy-done
  655.4 1.0 fusion.26
  656.4 0.1 fusion.51
  656.5 0.1 copy.52
  656.6 1.5 custom-call.12
  658.1 0.6 compare_reduce_fusion.3
  658.8 0.6 select_select_fusion.3
  659.4 1.2 custom-call.13
  660.6 0.2 fusion.39
  660.8 1.0 fusion.24
  661.8 0.1 fusion.52
  662.0 0.1 copy.54
  662.1 1.5 custom-call.14
  663.6 0.6 compare_reduce_fusion.2
  664.2 0.6 select_select_fusion.2
  664.9 1.2 custom-call.15
  666.1 0.2 fusion.37
  666.3 1.0 fusion.22
  667.3 0.1 fusion.53
  667.5 0.1 copy.56
  667.5 1.5 custom-call.16
  669.0 0.6 compare_reduce_fusion.1
  669.7 0.6 select_select_fusion.1
  670.3 1.2 custom-call.17
  671.6 0.2 fusion.35
  671.8 1.0 fusion.20
  672.8 0.1 fusion.54
  672.9 0.1 copy.58
  673.0 1.5 custom-call.18
  674.5 0.6 compare_reduce_fusion
  675.2 0.6 select_select_fusion
  675.8 1.2 custom-call.19
  677.0 0.2 fusion.7
  677.2 0.9 stack.6
  678.1 6.2 all-to-all-start.1
  684.3 0.9 convolution_convert_fusion.4
  685.2 293.9 %all-gather = bf16[2048,128]{1,0:T(8,128)(2,1)S(1)} all-gather(bf16[16,128]{1,0:T(8,128)(2,1)S(1)} %convolution_convert_fusion.4), channel_id=2, replica_groups=mesh['dom'=128,'ord'=2] {'dom'}, dimensions={0}, use_global_device_ids=true | all-gather | bytes 528384 | tf_op jit(solution)/shard_map/all_gather | solution.py:82
  979.1 0.0 all-to-all-done.1
  979.1 1.3 convolution_convert_fusion.1
  980.4 1.3 copy.59
  981.7 158.7 %all_to_all.35 = bf16[8,128,256]{2,1,0:T(8,128)(2,1)S(1)} all-to-all(bf16[8,128,256]{2,1,0:T(8,128)(2,1)S(1)} %copy.59), channel_id=1, replica_groups=mesh['dom'=128,'ord'=2] {'ord'}, dimensions={0} | all-to-all | bytes 1048576 | tf_op jit(solution)/shard_map/all_to_all | solution.py:91
  1140.5 0.5 copy.60
  1141.0 0.1 copy.68
  1141.1 1.2 convolution_convert_fusion
  (12 shorter events, 0.2 us)
Async XLA Ops:
  6.5 648.9 %copy-start = (f32[128,16,128]{2,1,0:T(8,128)S(1)}, f32[128,16,128]{2,1,0:T(8,128)}, u32[]{:S(2)}) copy-start(f32[128,16,128]{2,1,0:T(8,128)} %param.14) | copy-start | bytes 3145732
  6.5 13.1 %copy-start.3 = (s32[128]{0:T(128)S(1)}, s32[128]{0:T(128)}, u32[]{:S(2)}) copy-start(s32[128]{0:T(128)} %param.11) | copy-start | bytes 1540
  6.5 14.7 %copy-start.2 = (s32[128]{0:T(128)S(1)}, s32[128]{0:T(128)}, u32[]{:S(2)}) copy-start(s32[128]{0:T(128)} %param.12) | copy-start | bytes 1540
  13.0 8.1 all-to-all-start
  19.6 635.7 %reduce-scatter.2.cloned.1.call-start = ((), (), s32[]{:S(2)}) async-start(), calls=%async_computation.4 | async-start | bytes 8454144 | tf_op jit(solution)/shard_map/reduce_scatter | solution.py:71
  27.4 2.0 copy-start.1
  678.1 300.9 %all-to-all-start.1 = ((bf16[128,1,16,128]{3,2,1,0:T(8,128)(2,1)}), bf16[128,1,16,128]{3,2,1,0:T(8,128)(2,1)S(1)}, u32[]{:S(2)}, u32[]{:S(2)}) async-start(bf16[128,1,16,128]{3,2,1,0:T(8,128)(2,1)} %stack.6), calls=%async_computation.2 | async-start | bytes 1048576 | tf_op jit(solution)/shard_map/all_to_all | solution.py:80
Sparse Core Ops, SparseCore 0:
  35.2 620.1 reduce-scatter.1
